TPU v7x, 32 devices: a whole 2x2x4 slice. The times are simulated.
32 devices in a mesh: req: 4 (over z), mlp: 8 (over y, x, core).
Axes of the slice: x: 2, y: 2, z: 4, core: 2. Of those that a mesh axis runs over, the one named last changes fastest.
Arguments:
- tokens: bfloat16 [1024, 5120], P(('req', 'mlp')), may hold values from -6 to 6
- modulation: float32 [16, 6, 5120], P('req'), may hold values from -3 to 3
- lengths: int32 [4, 4], P('req'), may hold values from 1 to 160, 256 in all within a row
- request_adapter: int32 [16], P('req'), may hold values from 0 to 31
- adapter_storage: int32 [32], replicated, may hold values from 0 to 31, each once
- adapter_down_weight: bfloat16 [32, 5120, 32], P('mlp'), may hold values from -0.078125 to 0.078125
- adapter_up_maps: bfloat16 [32, 2, 16, 4096], P('mlp'), may hold values from -1.5 to 1.5
- input_projection: bfloat16 [4, 5120, 4096], P(None, None, 'mlp'), may hold values from -0.078125 to 0.078125
- query_key_gains: float32 [3, 4096], P(None, 'mlp'), may hold values from 0.1 to 1.9
- positions: int32 [3, 1024], P(None, 'req'), may hold values from 0 to 63
- block_page_lookup: int32 [4, 16], P('req'), may hold values from 0 to 15, each once within a row
- output_projection: bfloat16 [2, 4096, 5120], P(None, 'mlp'), may hold values from -0.09375 to 0.09375
- cross_norm_gain: float32 [5120], replicated, may hold values from 0.1 to 1.9
- text_token_cache: bfloat16 [2, 16, 512, 4096], P(None, 'req', None, 'mlp'), may hold values from -3 to 3
- feedforward_up: bfloat16 [5120, 8192], P('req', 'mlp'), may hold values from -0.078125 to 0.078125
- feedforward_down: bfloat16 [8192, 5120], P('mlp', 'req'), may hold values from -0.0625 to 0.0625
Outputs:
- layer_out: bfloat16 [1024, 5120], P(('req', 'mlp'))
- kv_pages: bfloat16 [2, 64, 16, 4096], P(None, 'req', None, 'mlp')
Inputs may be any that keep to these rules, and one draw needn't show every extreme that they name: `lengths`: row g lists the token counts of the 4 requests of group g in order; they fill the group's 256 positions, and the largest is 160. A permutation: adapter a is stored at index adapter_storage[a] of adapter_down_weight and adapter_up_maps. `block_page_lookup`: each row is a permutation of a group's 16 pages.
All inputs are finite; a program needn't handle non-finite values.
Results may differ from a plain program's by a relative error of at most 0.017.
Values may be sent and summed in bfloat16 or wider, within the bound.
A program may use at most 192 MiB of HBM per device.

v0:
```python
import math
import jax
import jax.numpy as jnp
from jax import lax
from jax.sharding import PartitionSpec as P

HD = 128
PAGE = 16
EPSILON = 1e-06


def as_sent(array):

    def short(part):
        return part.astype(jnp.bfloat16) if part.dtype == jnp.float32 else part

    return jax.tree.map(short, array)


def layer_norm(values):
    center = values - jnp.mean(values, axis=-1, keepdims=True)
    spread = jnp.mean(center * center, axis=-1, keepdims=True)
    return center * lax.rsqrt(spread + EPSILON)


def rotary_tables(grid):
    half_dim = HD // 2
    spatial = half_dim // 3
    temporal = half_dim - 2 * spatial
    column = jnp.arange(half_dim, dtype=jnp.int32)
    which_axis = jnp.where(
        column < temporal, 0, jnp.where(column < temporal + spatial, 1, 2)
    ).astype(jnp.int32)
    offset = jnp.where(
        which_axis == 0, 0, jnp.where(which_axis == 1, temporal, temporal + spatial)
    ).astype(jnp.int32)
    span_size = jnp.where(which_axis == 0, temporal, spatial).astype(jnp.float32)
    frequency = jnp.exp(-(column - offset).astype(jnp.float32) / span_size * math.log(10000.0))
    coordinate = grid.astype(jnp.float32)[which_axis, :].T
    angles = coordinate * frequency[None, :]
    return (jnp.cos(angles), jnp.sin(angles))


def rotate(values, cosine, sine_part):
    half_dim = HD // 2
    front_half = values[..., :half_dim]
    back_half = values[..., half_dim:]
    cosine = cosine[:, None, :]
    sine_part = sine_part[:, None, :]
    return jnp.concatenate(
        [front_half * cosine - back_half * sine_part, back_half * cosine + front_half * sine_part],
        axis=-1,
    )


def attend(queries, key_rows, value_rows, allowed):
    scores = jnp.einsum(
        "thd,shd->hts", queries, key_rows, preferred_element_type=jnp.float32
    ) / math.sqrt(HD)
    scores = jnp.where(allowed[None], scores, -1e30)
    weights = jnp.exp(scores)
    weights = (weights / jnp.sum(weights, axis=-1, keepdims=True)).astype(jnp.bfloat16)
    return jnp.einsum(
        "hts,shd->thd", weights, value_rows, preferred_element_type=jnp.float32
    ).astype(jnp.bfloat16)


def choose_rows(table, segment):
    chosen = jnp.zeros((segment.shape[0],) + table.shape[1:], table.dtype)
    for request in range(table.shape[0]):
        picked = (segment == request).reshape((-1,) + (1,) * (table.ndim - 1))
        chosen = jnp.where(picked, table[request][None], chosen)
    return chosen


def body(
    tokens,
    modulation,
    lengths,
    request_adapter,
    adapter_storage,
    adapter_down_weight,
    adapter_up_maps,
    input_projection,
    query_key_gains,
    positions,
    block_page_lookup,
    output_projection,
    cross_norm_gain,
    text_token_cache,
    feedforward_up,
    feedforward_down,
):
    mlp_count = lax.axis_size("mlp")
    my_index = lax.axis_index("mlp")
    own_count = tokens.shape[0]
    group_rows = own_count * mlp_count
    local_width = input_projection.shape[2]
    heads_local = local_width // HD
    entire_width = local_width * mlp_count
    resident_slots = adapter_down_weight.shape[0]
    doubled_rank = adapter_down_weight.shape[2]
    rank_once = doubled_rank // 2

    def over_group(own_rows, row_fn):
        return row_fn(lax.all_gather(own_rows, "mlp", axis=0, tiled=True), jnp.int32(0))

    def sum_rows(term_fn):
        return lax.psum_scatter(
            term_fn(jnp.int32(0), own_count * lax.axis_size("mlp")).astype(jnp.bfloat16),
            "mlp",
            scatter_dimension=0,
            tiled=True,
        ).astype(jnp.float32)

    def global_sum(pieces):
        return jax.tree.map(lambda part: part.astype(jnp.float32), lax.psum(as_sent(pieces), "mlp"))

    up_full, down_full = (
        lax.all_gather(feedforward_up, "req", axis=0, tiled=True),
        lax.all_gather(feedforward_down, "req", axis=1, tiled=True),
    )
    adapter_up_weight = lax.all_to_all(
        adapter_up_maps, "mlp", split_axis=3, concat_axis=0, tiled=True
    )
    slot_total = adapter_up_weight.shape[0]
    bounds = jnp.cumsum(lengths[0])
    position = jnp.arange(group_rows, dtype=jnp.int32)
    segment = jnp.sum((position[:, None] >= bounds[None, :]).astype(jnp.int32), axis=1)
    own_start = my_index * own_count
    own_segment = lax.dynamic_slice_in_dim(segment, own_start, own_count)
    per_token = [choose_rows(modulation[:, which_row, :], own_segment) for which_row in range(6)]
    token_f32 = tokens.astype(jnp.float32)
    normed_in = (layer_norm(token_f32) * (1.0 + per_token[1]) + per_token[0]).astype(jnp.bfloat16)

    def project_rows(incoming_rows, row_start):
        row_total = incoming_rows.shape[0]
        parts = [
            jnp.dot(incoming_rows, input_projection[which_map], preferred_element_type=jnp.float32)
            for which_map in range(3)
        ]
        code_block = jnp.einsum(
            "lf,sfe->lse", incoming_rows, adapter_down_weight, preferred_element_type=jnp.float32
        )
        parts.append(code_block.reshape(row_total, resident_slots * doubled_rank))
        return jnp.concatenate(parts, axis=1)

    projected = over_group(normed_in, project_rows)
    query_base = projected[:, :local_width]
    key_linear = projected[:, local_width : 2 * local_width]
    value_base = projected[:, 2 * local_width : 3 * local_width]
    code_block = projected[:, 3 * local_width :].reshape(group_rows, resident_slots, doubled_rank)
    request_slot = adapter_storage[request_adapter]
    token_slot = choose_rows(request_slot, segment)
    held = (
        token_slot[:, None]
        == my_index * resident_slots + jnp.arange(resident_slots, dtype=jnp.int32)[None, :]
    ).astype(jnp.float32)
    my_codes = jnp.sum(held[:, :, None] * code_block, axis=1)
    codes = global_sum(my_codes).astype(jnp.bfloat16)
    everywhere = (token_slot[:, None] == jnp.arange(slot_total, dtype=jnp.int32)[None, :]).astype(
        jnp.float32
    )

    def spread(code_part):
        return (
            (everywhere[:, :, None] * code_part[:, None, :].astype(jnp.float32))
            .reshape(group_rows, slot_total * rank_once)
            .astype(jnp.bfloat16)
        )

    query_up_weight = adapter_up_weight[:, 0].reshape(slot_total * rank_once, local_width)
    value_up_weight = adapter_up_weight[:, 1].reshape(slot_total * rank_once, local_width)
    query_linear = query_base + jnp.dot(
        spread(codes[:, :rank_once]), query_up_weight, preferred_element_type=jnp.float32
    )
    value_rows = (
        value_base
        + jnp.dot(spread(codes[:, rank_once:]), value_up_weight, preferred_element_type=jnp.float32)
    ).astype(jnp.bfloat16)
    query_square, key_square = global_sum(
        (jnp.sum(query_linear * query_linear, axis=1), jnp.sum(key_linear * key_linear, axis=1))
    )
    query_norm = (
        query_linear
        * lax.rsqrt(query_square / entire_width + EPSILON)[:, None]
        * query_key_gains[0]
    )
    key_norm = (
        key_linear * lax.rsqrt(key_square / entire_width + EPSILON)[:, None] * query_key_gains[1]
    )
    cosine, sine_part = rotary_tables(positions)
    query_rot = rotate(query_norm.reshape(group_rows, heads_local, HD), cosine, sine_part).astype(
        jnp.bfloat16
    )
    key_rot = rotate(key_norm.reshape(group_rows, heads_local, HD), cosine, sine_part).astype(
        jnp.bfloat16
    )
    value_heads = value_rows.reshape(group_rows, heads_local, HD)
    page_count = group_rows // PAGE
    stacked = jnp.stack(
        [
            key_rot.reshape(page_count, PAGE, local_width),
            value_rows.reshape(page_count, PAGE, local_width),
        ]
    )
    kv_pages = jnp.zeros_like(stacked).at[:, block_page_lookup[0]].set(stacked)
    allowed = segment[:, None] == segment[None, :]
    attended = attend(query_rot, key_rot, value_heads, allowed).reshape(group_rows, local_width)
    text_owner = (
        jnp.arange(text_token_cache.shape[1] * text_token_cache.shape[2], dtype=jnp.int32)
        // text_token_cache.shape[2]
    )
    cross_allowed = segment[:, None] == text_owner[None, :]
    text_keys = text_token_cache[0].reshape(-1, heads_local, HD)
    text_values = text_token_cache[1].reshape(-1, heads_local, HD)

    def attend_term(row_start, row_total):
        return jnp.dot(attended, output_projection[0], preferred_element_type=jnp.float32)

    first_res = (token_f32 + per_token[2] * sum_rows(attend_term)).astype(jnp.bfloat16)
    cross_own = (layer_norm(first_res.astype(jnp.float32)) * cross_norm_gain).astype(jnp.bfloat16)

    def cross_rows(incoming_rows, row_start):
        return jnp.dot(incoming_rows, input_projection[3], preferred_element_type=jnp.float32)

    cross_linear = over_group(cross_own, cross_rows)
    cross_square = global_sum(jnp.sum(cross_linear * cross_linear, axis=1))
    cross_query = (
        cross_linear
        * lax.rsqrt(cross_square / entire_width + EPSILON)[:, None]
        * query_key_gains[2]
    ).astype(jnp.bfloat16)
    cross_out = attend(
        cross_query.reshape(group_rows, heads_local, HD), text_keys, text_values, cross_allowed
    ).reshape(group_rows, local_width)

    def cross_term(row_start, row_total):
        return jnp.dot(cross_out, output_projection[1], preferred_element_type=jnp.float32)

    second_res = (first_res.astype(jnp.float32) + sum_rows(cross_term)).astype(jnp.bfloat16)
    mlp_own = (
        layer_norm(second_res.astype(jnp.float32)) * (1.0 + per_token[4]) + per_token[3]
    ).astype(jnp.bfloat16)

    def expand_rows(incoming_rows, row_start):
        return jax.nn.gelu(
            jnp.dot(incoming_rows, up_full, preferred_element_type=jnp.float32), approximate=True
        ).astype(jnp.bfloat16)

    hidden = over_group(mlp_own, expand_rows)

    def down_term(row_start, row_total):
        return jnp.dot(hidden, down_full, preferred_element_type=jnp.float32)

    layer_out = (second_res.astype(jnp.float32) + per_token[5] * sum_rows(down_term)).astype(
        jnp.bfloat16
    )
    return (layer_out, kv_pages)


def solution(mesh):
    return jax.shard_map(
        body,
        mesh=mesh,
        in_specs=(
            P(("req", "mlp"), None),
            P("req", None, None),
            P("req", None),
            P("req"),
            P(),
            P("mlp", None, None),
            P("mlp", None, None, None),
            P(None, None, "mlp"),
            P(None, "mlp"),
            P(None, "req"),
            P("req", None),
            P(None, "mlp", None),
            P(),
            P(None, "req", None, "mlp"),
            P("req", "mlp"),
            P("mlp", "req"),
        ),
        out_specs=(P(("req", "mlp"), None), P(None, "req", None, "mlp")),
        check_vma=False,
    )
```

profile of v0, /device:TPU:0, one launch (start us, length us, event | category | flops | bytes accessed | tf_op | source)
XLA Modules:
  0.0 720.8 jit_solution(13914493310342817437)
XLA Ops:
  8.1 2.6 fusion.93
  14.1 2.1 fusion.51
  16.2 11.0 %copy.88 = bf16[4,2,16,4096]{2,0,1,3:T(4,128)(2,1)} copy(bf16[4,2,16,4096]{3,2,1,0:T(8,128)(2,1)} %param.22) | data formatting | bytes 2097152 | tf_op args[6]
  27.2 11.3 %reshape.439 = bf16[8,2,32768]{2,1,0:T(2,128)(2,1)} reshape(bf16[4096,2,4,16]{3,2,1,0:T(4,128)(2,1)} %bitcast.123) | data formatting | bytes 2097152
  38.5 5.2 all-to-all-start
  45.8 2.5 compare_select_fusion.10
  51.5 8.3 %all-to-all-done = bf16[8,2,32768]{2,1,0:T(2,128)(2,1)S(1)} async-done(((bf16[8,2,32768]{2,1,0:T(2,128)(2,1)}), bf16[8,2,32768]{2,1,0:T(2,128)(2,1)S(1)}, u32[]{:S(2)}, u32[]{:S(2)}) %all-to-all-start) | async-done | bytes 1048608 | tf_op jit(solution)/shard_map/all_to_all | solution.py:123
  59.8 7.6 %reshape.440 = bf16[4096,2,4,16]{3,2,1,0:T(4,128)(2,1)} reshape(bf16[8,2,32768]{2,1,0:T(2,128)(2,1)S(1)} %all-to-all-done) | data formatting | bytes 2097152
  67.3 10.8 %copy.106 = bf16[4,2,16,8,512]{4,2,1,0,3:T(8,128)(2,1)S(1)} copy(bf16[4,2,16,8,512]{2,0,1,4,3:T(4,128)(2,1)} %bitcast.122) | data formatting | bytes 2097152 | tf_op jit(solution)/shard_map/all_to_all | solution.py:123
  78.2 2.7 fusion.99
  81.0 22.3 %psum.28 = bf16[256,32]{0,1:T(8,128)(2,1)S(1)} all-reduce(bf16[256,32]{0,1:T(8,128)(2,1)S(1)} %multiply_reduce_fusion.3), channel_id=1, replica_groups=mesh['req'=4,'mlp'=8] {'mlp'}, use_global_device_ids=true, to_apply=%region_5.6 | all-reduce | flops 8192 | bytes 32768 | tf_op jit(solution)/shard_map/psum | solution.py:117
  104.9 4.9 fusion.7
  110.3 4.1 multiply_reduce_fusion.1
  114.4 12.0 %all-reduce = (bf16[256]{0:T(256)(128)(2,1)S(1)}, bf16[256]{0:T(256)(128)(2,1)S(1)}) all-reduce(bf16[256]{0:T(256)(128)(2,1)S(1)} %get-tuple-element.62, bf16[256]{0:T(256)(128)(2,1)S(1)} %get-tuple-element.64), channel_id=1, replica_groups=mesh['req'=4,'mlp'=8] {'mlp'}, use_global_device_ids=true, to_apply=%region_9.10 | all-reduce | flops 512 | bytes 2048 | tf_op jit(solution)/shard_map/psum | solution.py:117
  127.7 4.8 fusion.9
  136.1 5.6 convolution_convert_fusion.2
  142.9 42.6 %reduce-scatter.4.cloned.1.call-done = bf16[32,5120]{1,0:T(8,128)(2,1)} async-done(((bf16[256,5120]{1,0:T(8,128)(2,1)}), bf16[32,5120]{1,0:T(8,128)(2,1)}) %reduce-scatter.4.cloned.1.call-update) | async-done | bytes 327696 | tf_op jit(solution)/shard_map/reduce_scatter | solution.py:109
  188.1 4.0 fusion.89
  192.1 4.0 reshape_squeeze.14
  196.1 2.1 reshape.438
  198.6 19.7 %all-gather.8.cloned.1.call-done = bf16[256,5120]{1,0:T(8,128)(2,1)} async-done(((bf16[32,5120]{1,0:T(8,128)(2,1)}), bf16[256,5120]{1,0:T(8,128)(2,1)}) %all-gather.8.cloned.1.call-update) | async-done | bytes 2621456 | tf_op jit(solution)/shard_map/all_gather | solution.py:106
  218.3 5.6 multiply_reduce_fusion
  223.9 13.3 %psum.31 = bf16[256]{0:T(256)(128)(2,1)S(1)} all-reduce(bf16[256]{0:T(256)(128)(2,1)S(1)} %get-tuple-element.66), channel_id=1, replica_groups=mesh['req'=4,'mlp'=8] {'mlp'}, use_global_device_ids=true, to_apply=%region_15.16 | all-reduce | flops 256 | bytes 1024 | tf_op jit(solution)/shard_map/psum | solution.py:117
  237.3 6.4 fusion
  243.6 5.9 fusion.24
  249.6 3.1 convolution_convert_fusion.1
  254.0 42.6 %reduce-scatter.6.cloned.1.call-done = bf16[32,5120]{1,0:T(8,128)(2,1)} async-done(((bf16[256,5120]{1,0:T(8,128)(2,1)}), bf16[32,5120]{1,0:T(8,128)(2,1)}) %reduce-scatter.6.cloned.1.call-update) | async-done | bytes 327696 | tf_op jit(solution)/shard_map/reduce_scatter | solution.py:109
  299.6 139.0 %all-gather.12.cloned.1.call-done = bf16[5120,1024]{1,0:T(8,128)(2,1)} async-done(((bf16[1280,1024]{1,0:T(8,128)(2,1)}), bf16[5120,1024]{1,0:T(8,128)(2,1)}) %all-gather.12.cloned.1.call-update) | async-done | bytes 10485776 | tf_op jit(solution)/shard_map/all_gather | solution.py:120
  438.6 183.4 %all-gather.14.cloned.1.call-done = bf16[1024,5120]{1,0:T(8,128)(2,1)} async-done(((bf16[1024,1280]{1,0:T(8,128)(2,1)}), bf16[1024,5120]{1,0:T(8,128)(2,1)}) %all-gather.14.cloned.1.call-update) | async-done | bytes 10485776 | tf_op jit(solution)/shard_map/all_gather | solution.py:121
  622.0 30.5 %all-gather.10.cloned.1.call-done = bf16[256,5120]{1,0:T(8,128)(2,1)} async-done(((bf16[32,5120]{1,0:T(8,128)(2,1)}), bf16[256,5120]{1,0:T(8,128)(2,1)}) %all-gather.10.cloned.1.call-update) | async-done | bytes 2621456 | tf_op jit(solution)/shard_map/all_gather | solution.py:106
  652.5 15.1 %convolution_convert_fusion = bf16[256,5120]{1,0:T(8,128)(2,1)} fusion(bf16[1024,5120]{1,0:T(8,128)(2,1)} %all-gather.14.cloned.1.call-done, bf16[256,5120]{1,0:T(8,128)(2,1)} %all-gather.10.cloned.1.call-done, bf16[5120,1024]{1,0:T(8,128)(2,1)} %all-gather.12.cloned.1.call-done), kind=kOutput, calls=%fused_computation.6 | convolution fusion | flops 5372379136 | bytes 26214400 | tf_op jit(solution)/shard_map/dot_general | solution.py:254
  669.5 42.0 %reduce-scatter.8.cloned.1.call-done = bf16[32,5120]{1,0:T(8,128)(2,1)} async-done(((bf16[256,5120]{1,0:T(8,128)(2,1)}), bf16[32,5120]{1,0:T(8,128)(2,1)}) %reduce-scatter.8.cloned.1.call-update) | async-done | bytes 327696 | tf_op jit(solution)/shard_map/reduce_scatter | solution.py:109
  (166 shorter events, 27.4 us)
Async XLA Ops:
  8.0 70.2 %copy-start = (bf16[4,5120,32]{1,2,0:T(8,128)(2,1)S(1)}, bf16[4,5120,32]{1,2,0:T(8,128)(2,1)}, u32[]{:S(2)}) copy-start(bf16[4,5120,32]{1,2,0:T(8,128)(2,1)} %param.21) | copy-start | bytes 3932164
  8.0 70.2 %all-gather.6.cloned.1.call-start = ((), (), s32[]{:S(2)}) async-start(), calls=%async_computation.4 | async-start | bytes 2949120 | tf_op jit(solution)/shard_map/all_gather | solution.py:106
  38.5 21.3 %all-to-all-start = ((bf16[8,2,32768]{2,1,0:T(2,128)(2,1)}), bf16[8,2,32768]{2,1,0:T(2,128)(2,1)S(1)}, u32[]{:S(2)}, u32[]{:S(2)}) async-start(bf16[8,2,32768]{2,1,0:T(2,128)(2,1)} %reshape.439), calls=%async_computation | async-start | bytes 2097152 | tf_op jit(solution)/shard_map/all_to_all | solution.py:123
  43.7 141.8 %reduce-scatter.4.cloned.1.call-start = ((), (), s32[]{:S(2)}) async-start(), calls=%async_computation.5 | async-start | bytes 2949120 | tf_op jit(solution)/shard_map/reduce_scatter | solution.py:109
  136.0 49.5 %copy-start.3 = (bf16[32,5120]{1,0:T(8,128)(2,1)S(1)}, bf16[32,5120]{1,0:T(8,128)(2,1)}, u32[]{:S(2)}) copy-start(bf16[32,5120]{1,0:T(8,128)(2,1)} %param.16) | copy-start | bytes 983044
  136.0 49.4 %copy-start.25 = (f32[1,1,5120]{2,0,1:T(1,128)S(1)}, f32[1,1,5120]{2,0,1:T(1,128)}, u32[]{:S(2)}) copy-start(f32[1,1,5120]{2,0,1:T(1,128)} %get-tuple-element.40) | copy-start | bytes 61444
  136.0 49.4 %copy-start.28 = (pred[32]{0:T(512)(128)(4,1)S(1)}, pred[32]{0:T(512)(128)(4,1)}, u32[]{:S(2)}) copy-start(pred[32]{0:T(512)(128)(4,1)} %copy-done.27) | copy-start | bytes 100
  136.0 49.4 %copy-start.30 = (pred[32]{0:T(512)(128)(4,1)S(1)}, pred[32]{0:T(512)(128)(4,1)}, u32[]{:S(2)}) copy-start(pred[32]{0:T(512)(128)(4,1)} %copy-done.29) | copy-start | bytes 100
  136.1 51.1 %copy-start.26 = (f32[5120]{0:T(1024)S(1)}, f32[5120]{0:T(1024)}, u32[]{:S(2)}) copy-start(f32[5120]{0:T(1024)} %param.28) | copy-start | bytes 61444
  141.7 76.6 %all-gather.8.cloned.1.call-start = ((), (), s32[]{:S(2)}) async-start(), calls=%async_computation.6 | async-start | bytes 2949120 | tf_op jit(solution)/shard_map/all_gather | solution.py:106
  188.1 108.6 %reduce-scatter.6.cloned.1.call-start = ((), (), s32[]{:S(2)}) async-start(), calls=%async_computation.7 | async-start | bytes 2949120 | tf_op jit(solution)/shard_map/reduce_scatter | solution.py:109
  198.6 38.6 %copy-start.10 = (bf16[2048,4,128]{2,1,0:T(4,128)(2,1)S(1)}, bf16[2048,4,128]{2,1,0:T(4,128)(2,1)}, u32[]{:S(2)}) copy-start(bf16[2048,4,128]{2,1,0:T(4,128)(2,1)} %reshape_squeeze.14) | copy-start | bytes 6291460
  198.6 38.6 %copy-start.35 = (f32[1,512]{1,0:T(1,128)S(1)}, f32[1,512]{1,0:T(1,128)}, u32[]{:S(2)}) copy-start(f32[1,512]{1,0:T(1,128)} %get-tuple-element.52) | copy-start | bytes 6148
  252.7 45.3 %copy-start.15 = (f32[1,1,5120]{2,0,1:T(1,128)S(1)}, f32[1,1,5120]{2,0,1:T(1,128)}, u32[]{:S(2)}) copy-start(f32[1,1,5120]{2,0,1:T(1,128)} %get-tuple-element.23) | copy-start | bytes 61444
  252.7 45.3 %copy-start.16 = (f32[1,1,5120]{2,0,1:T(1,128)S(1)}, f32[1,1,5120]{2,0,1:T(1,128)}, u32[]{:S(2)}) copy-start(f32[1,1,5120]{2,0,1:T(1,128)} %get-tuple-element.24) | copy-start | bytes 61444
  252.7 45.4 %copy-start.17 = (f32[1,1,5120]{2,0,1:T(1,128)S(1)}, f32[1,1,5120]{2,0,1:T(1,128)}, u32[]{:S(2)}) copy-start(f32[1,1,5120]{2,0,1:T(1,128)} %get-tuple-element.25) | copy-start | bytes 61444
  252.7 45.4 %copy-start.18 = (f32[1,1,5120]{2,0,1:T(1,128)S(1)}, f32[1,1,5120]{2,0,1:T(1,128)}, u32[]{:S(2)}) copy-start(f32[1,1,5120]{2,0,1:T(1,128)} %get-tuple-element.26) | copy-start | bytes 61444
  252.8 45.4 %copy-start.19 = (f32[1,1,5120]{2,0,1:T(1,128)S(1)}, f32[1,1,5120]{2,0,1:T(1,128)}, u32[]{:S(2)}) copy-start(f32[1,1,5120]{2,0,1:T(1,128)} %get-tuple-element.27) | copy-start | bytes 61444
  252.8 45.4 %copy-start.20 = (f32[1,1,5120]{2,0,1:T(1,128)S(1)}, f32[1,1,5120]{2,0,1:T(1,128)}, u32[]{:S(2)}) copy-start(f32[1,1,5120]{2,0,1:T(1,128)} %get-tuple-element.28) | copy-start | bytes 61444
  252.8 185.8 %all-gather.12.cloned.1.call-start = ((), (), s32[]{:S(2)}) async-start(), calls=%async_computation.9 | async-start | bytes 13107200 | tf_op jit(solution)/shard_map/all_gather | solution.py:120
  253.4 368.7 %all-gather.14.cloned.1.call-start = ((), (), s32[]{:S(2)}) async-start(), calls=%async_computation.10 | async-start | bytes 13107200 | tf_op jit(solution)/shard_map/all_gather | solution.py:121
  254.0 398.6 %all-gather.10.cloned.1.call-start = ((), (), s32[]{:S(2)}) async-start(), calls=%async_computation.8 | async-start | bytes 2949120 | tf_op jit(solution)/shard_map/all_gather | solution.py:106
  299.3 368.4 %copy-start.37 = (s32[1,16]{1,0:T(1,128)S(1)}, s32[1,16]{1,0:T(1,128)}, u32[]{:S(2)}) copy-start(s32[1,16]{1,0:T(1,128)} %param.26) | copy-start | bytes 196
  299.3 368.4 %copy-start.8 = (bf16[256,4,128]{2,0,1:T(8,128)(2,1)S(1)}, bf16[256,4,128]{2,0,1:T(8,128)(2,1)}, u32[]{:S(2)}) copy-start(bf16[256,4,128]{2,0,1:T(8,128)(2,1)} %copy-done.7) | copy-start | bytes 786436
  299.3 368.8 %copy-start.6 = (bf16[256,512]{1,0:T(8,128)(2,1)S(1)}, bf16[256,512]{1,0:T(8,128)(2,1)}, u32[]{:S(2)}) copy-start(bf16[256,512]{1,0:T(8,128)(2,1)} %copy-done.5) | copy-start | bytes 786436
  299.3 412.2 %reduce-scatter.8.cloned.1.call-start = ((), (), s32[]{:S(2)}) async-start(), calls=%async_computation.11 | async-start | bytes 2949120 | tf_op jit(solution)/shard_map/reduce_scatter | solution.py:109
  652.5 61.0 %copy-start.1 = (bf16[4,5120,32]{1,2,0:T(8,128)(2,1)S(1)}, bf16[4,5120,32]{1,2,0:T(8,128)(2,1)}, u32[]{:S(2)}) copy-start(bf16[4,5120,32]{1,2,0:T(8,128)(2,1)} %param.21) | copy-start | bytes 3932164
  667.7 43.8 %copy-start.21 = (f32[1,1,5120]{2,0,1:T(1,128)S(1)}, f32[1,1,5120]{2,0,1:T(1,128)}, u32[]{:S(2)}) copy-start(f32[1,1,5120]{2,0,1:T(1,128)} %get-tuple-element.22) | copy-start | bytes 61444
  667.7 43.8 %copy-start.22 = (f32[1,1,5120]{2,0,1:T(1,128)S(1)}, f32[1,1,5120]{2,0,1:T(1,128)}, u32[]{:S(2)}) copy-start(f32[1,1,5120]{2,0,1:T(1,128)} %get-tuple-element.29) | copy-start | bytes 61444
  667.7 43.8 %copy-start.23 = (f32[1,1,5120]{2,0,1:T(1,128)S(1)}, f32[1,1,5120]{2,0,1:T(1,128)}, u32[]{:S(2)}) copy-start(f32[1,1,5120]{2,0,1:T(1,128)} %get-tuple-element.30) | copy-start | bytes 61444
  667.7 43.9 %copy-start.24 = (f32[1,1,5120]{2,0,1:T(1,128)S(1)}, f32[1,1,5120]{2,0,1:T(1,128)}, u32[]{:S(2)}) copy-start(f32[1,1,5120]{2,0,1:T(1,128)} %get-tuple-element.31) | copy-start | bytes 61444
  669.5 44.0 %copy-start.11 = (bf16[2,16,16,512]{3,2,1,0:T(8,128)(2,1)}, bf16[2,16,16,512]{3,2,1,0:T(8,128)(2,1)S(1)}, u32[]{:S(2)}) copy-start(bf16[2,16,16,512]{3,2,1,0:T(8,128)(2,1)S(1)} %scatter_fusion) | copy-start | bytes 1572868
  (18 other events, 189.5 us)
Sparse Core Ops, SparseCore 0:
  16.3 33.5 all-gather.5
  141.8 43.6 reduce-scatter.3
  188.2 30.0 all-gather.7
  252.9 43.6 reduce-scatter.5
  667.8 43.6 reduce-scatter.7
Sparse Core Ops, SparseCore 1:
  254.8 183.7 all-gather.11
  440.1 181.9 all-gather.13
  624.4 28.1 all-gather.9
where the time goes:
time: 723 us; the launch traced here: 721 us
  waiting for transfers between devices  509 us (70%)
  local copies, waits for them, and re-layouts  61.7 us (9%)
  matrix products  60.8 us (8%)
  blocking collectives  47.6 us (7%)
  other arithmetic  19.5 us (3%)
  between operations  16.2 us (2%)
    all_gather x1, waiting for transfers between devices, body(): lax.all_gather(feedforward_down, 'req', axis=1, tiled=True)  183 us
    all_gather x1, waiting for transfers between devices, body(): lax.all_gather(feedforward_up, 'req', axis=0, tiled=True)  139 us
    reduce_scatter x3, waiting for transfers between devices, sum_rows(): lax.psum_scatter(term_fn(jnp.int32(0), own_count * lax.axis_size('mlp'))....  127 us
    all_gather x3, waiting for transfers between devices, over_group(): lax.all_gather(own_rows, 'mlp', axis=0, tiled=True)  50.2 us
    psum x3, blocking collectives, global_sum(): lax.psum(as_sent(pieces), 'mlp')  47.6 us
    unnamed x85, local copies, waits for them, and re-layouts  30 us
    dot_general x1, matrix products, down_term(): return jnp.dot(hidden, down_full, preferred_element_type=jnp.float32)  15.1 us
  transfers between devices with their start and end apart: 9, of which 8 were waited for; matrix products, arithmetic and copies ran while one was open for 9% of the time, Pallas kernels for 0%

commit v1 on v0

--- a/solution.py
+++ b/solution.py
@@ -7,6 +7,18 @@
 HD = 128
 PAGE = 16
 EPSILON = 1e-06
+
+
+def cut_along(x, dim, size):
+    shape = x.shape
+    blocks = x.reshape(*shape[:dim], size, shape[dim] // size, *shape[dim + 1 :])
+    return jnp.moveaxis(blocks, dim, 0)
+
+
+def laid_out(blocks, dim):
+    shape = list(blocks.shape[1:])
+    shape[dim] *= blocks.shape[0]
+    return jnp.moveaxis(blocks, 0, dim).reshape(shape)
 
 
 def as_sent(array):
@@ -120,9 +132,14 @@
         lax.all_gather(feedforward_up, "req", axis=0, tiled=True),
         lax.all_gather(feedforward_down, "req", axis=1, tiled=True),
     )
-    adapter_up_weight = lax.all_to_all(
-        adapter_up_maps, "mlp", split_axis=3, concat_axis=0, tiled=True
-    )
+    length, here = (lax.axis_size("mlp"), lax.axis_index("mlp"))
+    blocks = cut_along(adapter_up_maps, 3, length)
+    finished = [blocks[here]]
+    for hop in range(1, length):
+        sent = blocks[here ^ hop]
+        finished.append(lax.ppermute(sent, "mlp", [(i, i ^ hop) for i in range(length)]))
+    blocks = jnp.stack(finished)[here ^ jnp.arange(length)]
+    adapter_up_weight = laid_out(blocks, 0)
     slot_total = adapter_up_weight.shape[0]
     bounds = jnp.cumsum(lengths[0])
     position = jnp.arange(group_rows, dtype=jnp.int32)

time: 723 us -> 701 us (0.970)
  local copies, waits for them, and re-layouts: 61.7 us -> 35.2 us
    unnamed x85 -> x103, local copies, waits for them, and re-layouts: 30 us -> 10.6 us
    all_to_all x1 -> x0, local copies, waits for them, and re-layouts: 10.8 us -> none  [body(): lax.all_to_all(adapter_up_maps, 'mlp', split_axis=3, concat_axis=0, tiled...]
    all_to_all x1 -> x0, waiting for transfers between devices: 8.27 us -> none  [body(): lax.all_to_all(adapter_up_maps, 'mlp', split_axis=3, concat_axis=0, tiled...]
    ppermute x0 -> x7, starting transfers between devices: none -> 7.8 us  [body(): lax.ppermute(sent, 'mlp', [(i, i ^ hop) for i in range(length)])]
    ppermute x0 -> x7, waiting for transfers between devices: none -> 7.36 us  [body(): lax.ppermute(sent, 'mlp', [(i, i ^ hop) for i in range(length)])]
  transfers between devices with their start and end apart: 9 -> 15, of which waited for: 8 -> 10; matrix products, arithmetic and copies ran while one was open for 9% -> 5% of each run, Pallas kernels for 0% -> 0%
where the time goes in v1:
time: 701 us; the launch traced here: 700 us
  waiting for transfers between devices  511 us (73%)
  matrix products  59.8 us (9%)
  blocking collectives  49.9 us (7%)
  local copies, waits for them, and re-layouts  35.2 us (5%)
  other arithmetic  19.3 us (3%)
  between operations  16.4 us (2%)
  starting transfers between devices  8.39 us (1%)
    all_gather x1, waiting for transfers between devices, body(): lax.all_gather(feedforward_down, 'req', axis=1, tiled=True)  183 us
    all_gather x1, waiting for transfers between devices, body(): lax.all_gather(feedforward_up, 'req', axis=0, tiled=True)  139 us
    reduce_scatter x3, waiting for transfers between devices, sum_rows(): lax.psum_scatter(term_fn(jnp.int32(0), own_count * lax.axis_size('mlp'))....  127 us
    all_gather x3, waiting for transfers between devices, over_group(): lax.all_gather(own_rows, 'mlp', axis=0, tiled=True)  53.3 us
    psum x3, blocking collectives, global_sum(): lax.psum(as_sent(pieces), 'mlp')  49.9 us
    dot_general x1, matrix products, down_term(): return jnp.dot(hidden, down_full, preferred_element_type=jnp.float32)  15 us
  transfers between devices with their start and end apart: 15, of which 10 were waited for; matrix products, arithmetic and copies ran while one was open for 5% of the time, Pallas kernels for 0%

profile of v1, /device:TPU:0, one launch (start us, length us, event | category | flops | bytes accessed | tf_op | source)
XLA Modules:
  0.0 699.7 jit_solution(7017948126107459432)
XLA Ops:
  9.2 2.7 fusion.94
  14.2 2.1 fusion.51
  18.1 3.1 constant_dynamic-slice_fusion
  22.3 2.6 collective-permute-start.1
  29.1 2.4 compare_select_fusion.11
  38.6 2.5 collective-permute-start.5
  47.7 5.5 collective-permute-done.6
  54.1 3.0 all-gather.6.cloned.1.call-done
  57.1 2.7 fusion.100
  59.9 24.6 %psum.28 = bf16[256,32]{0,1:T(8,128)(2,1)S(1)} all-reduce(bf16[256,32]{0,1:T(8,128)(2,1)S(1)} %multiply_reduce_fusion.3), channel_id=1, replica_groups=mesh['req'=4,'mlp'=8] {'mlp'}, use_global_device_ids=true, to_apply=%region_5.6 | all-reduce | flops 8192 | bytes 32768 | tf_op jit(solution)/shard_map/psum | solution.py:129
  85.3 4.9 fusion.7
  90.7 4.1 multiply_reduce_fusion.1
  94.8 12.0 %all-reduce = (bf16[256]{0:T(256)(128)(2,1)S(1)}, bf16[256]{0:T(256)(128)(2,1)S(1)}) all-reduce(bf16[256]{0:T(256)(128)(2,1)S(1)} %get-tuple-element.70, bf16[256]{0:T(256)(128)(2,1)S(1)} %get-tuple-element.72), channel_id=1, replica_groups=mesh['req'=4,'mlp'=8] {'mlp'}, use_global_device_ids=true, to_apply=%region_9.10 | all-reduce | flops 512 | bytes 2048 | tf_op jit(solution)/shard_map/psum | solution.py:129
  108.1 4.8 fusion.9
  115.7 5.6 convolution_convert_fusion.2
  122.5 41.9 %reduce-scatter.4.cloned.1.call-done = bf16[32,5120]{1,0:T(8,128)(2,1)} async-done(((bf16[256,5120]{1,0:T(8,128)(2,1)}), bf16[32,5120]{1,0:T(8,128)(2,1)}) %reduce-scatter.4.cloned.1.call-update) | async-done | bytes 327696 | tf_op jit(solution)/shard_map/reduce_scatter | solution.py:121
  167.0 4.0 fusion.90
  171.0 4.0 reshape_squeeze.14
  174.9 2.1 reshape.485
  177.4 19.8 %all-gather.8.cloned.1.call-done = bf16[256,5120]{1,0:T(8,128)(2,1)} async-done(((bf16[32,5120]{1,0:T(8,128)(2,1)}), bf16[256,5120]{1,0:T(8,128)(2,1)}) %all-gather.8.cloned.1.call-update) | async-done | bytes 2621456 | tf_op jit(solution)/shard_map/all_gather | solution.py:118
  197.2 5.6 multiply_reduce_fusion
  202.8 13.3 %psum.31 = bf16[256]{0:T(256)(128)(2,1)S(1)} all-reduce(bf16[256]{0:T(256)(128)(2,1)S(1)} %get-tuple-element.74), channel_id=1, replica_groups=mesh['req'=4,'mlp'=8] {'mlp'}, use_global_device_ids=true, to_apply=%region_15.16 | all-reduce | flops 256 | bytes 1024 | tf_op jit(solution)/shard_map/psum | solution.py:129
  216.2 6.5 fusion
  222.6 5.9 fusion.24
  228.6 3.1 convolution_convert_fusion.1
  233.0 42.6 %reduce-scatter.6.cloned.1.call-done = bf16[32,5120]{1,0:T(8,128)(2,1)} async-done(((bf16[256,5120]{1,0:T(8,128)(2,1)}), bf16[32,5120]{1,0:T(8,128)(2,1)}) %reduce-scatter.6.cloned.1.call-update) | async-done | bytes 327696 | tf_op jit(solution)/shard_map/reduce_scatter | solution.py:121
  278.6 139.0 %all-gather.12.cloned.1.call-done = bf16[5120,1024]{1,0:T(8,128)(2,1)} async-done(((bf16[1280,1024]{1,0:T(8,128)(2,1)}), bf16[5120,1024]{1,0:T(8,128)(2,1)}) %all-gather.12.cloned.1.call-update) | async-done | bytes 10485776 | tf_op jit(solution)/shard_map/all_gather | solution.py:132
  417.6 183.4 %all-gather.14.cloned.1.call-done = bf16[1024,5120]{1,0:T(8,128)(2,1)} async-done(((bf16[1024,1280]{1,0:T(8,128)(2,1)}), bf16[1024,5120]{1,0:T(8,128)(2,1)}) %all-gather.14.cloned.1.call-update) | async-done | bytes 10485776 | tf_op jit(solution)/shard_map/all_gather | solution.py:133
  601.0 30.5 %all-gather.10.cloned.1.call-done = bf16[256,5120]{1,0:T(8,128)(2,1)} async-done(((bf16[32,5120]{1,0:T(8,128)(2,1)}), bf16[256,5120]{1,0:T(8,128)(2,1)}) %all-gather.10.cloned.1.call-update) | async-done | bytes 2621456 | tf_op jit(solution)/shard_map/all_gather | solution.py:118
  631.5 15.0 %convolution_convert_fusion = bf16[256,5120]{1,0:T(8,128)(2,1)} fusion(bf16[1024,5120]{1,0:T(8,128)(2,1)} %all-gather.14.cloned.1.call-done, bf16[256,5120]{1,0:T(8,128)(2,1)} %all-gather.10.cloned.1.call-done, bf16[5120,1024]{1,0:T(8,128)(2,1)} %all-gather.12.cloned.1.call-done), kind=kOutput, calls=%fused_computation.7 | convolution fusion | flops 5372379136 | bytes 26214400 | tf_op jit(solution)/shard_map/dot_general | solution.py:271
  648.4 42.1 %reduce-scatter.8.cloned.1.call-done = bf16[32,5120]{1,0:T(8,128)(2,1)} async-done(((bf16[256,5120]{1,0:T(8,128)(2,1)}), bf16[32,5120]{1,0:T(8,128)(2,1)}) %reduce-scatter.8.cloned.1.call-update) | async-done | bytes 327696 | tf_op jit(solution)/shard_map/reduce_scatter | solution.py:121
  690.4 2.0 fusion.54
  (200 shorter events, 40.1 us)
Async XLA Ops:
  8.0 49.1 %copy-start = (bf16[4,5120,32]{1,2,0:T(8,128)(2,1)S(1)}, bf16[4,5120,32]{1,2,0:T(8,128)(2,1)}, u32[]{:S(2)}) copy-start(bf16[4,5120,32]{1,2,0:T(8,128)(2,1)} %param.21) | copy-start | bytes 3932164
  8.0 49.1 %all-gather.6.cloned.1.call-start = ((), (), s32[]{:S(2)}) async-start(), calls=%async_computation.3 | async-start | bytes 2949120 | tf_op jit(solution)/shard_map/all_gather | solution.py:118
  16.4 148.0 %reduce-scatter.4.cloned.1.call-start = ((), (), s32[]{:S(2)}) async-start(), calls=%async_computation.4 | async-start | bytes 2949120 | tf_op jit(solution)/shard_map/reduce_scatter | solution.py:121
  21.9 16.7 %collective-permute-start = (bf16[4,2,16,512]{3,2,1,0:T(8,128)(2,1)}, bf16[4,2,16,512]{3,2,1,0:T(8,128)(2,1)}, u32[]{:S(2)}, u32[]{:S(2)}) collective-permute-start(bf16[4,2,16,512]{3,2,1,0:T(8,128)(2,1)} %bitcast.158), channel_id=1, source_target_pairs={{0,1},{1,0},{2,3},{3,2},{4,5},{5,4},{6,7},{7,6},{8,9},{9,8},{10,11... | collective-permute-start | bytes 393224 | tf_op jit(solution)/shard_map/ppermute | solution.py:140
  22.3 19.6 %collective-permute-start.1 = (bf16[4,2,16,512]{3,2,1,0:T(8,128)(2,1)S(1)}, bf16[4,2,16,512]{3,2,1,0:T(8,128)(2,1)}, u32[]{:S(2)}, u32[]{:S(2)}) collective-permute-start(bf16[4,2,16,512]{3,2,1,0:T(8,128)(2,1)S(1)} %bitcast.173), channel_id=1, source_target_pairs={{0,2},{1,3},{2,0},{3,1},{4,6},{5,7},{6,4},{7,5},{8,10},{9,11},{10,... | collective-permute-start | bytes 393224 | tf_op jit(solution)/shard_map/ppermute | solution.py:140
  24.9 18.2 %collective-permute-start.2 = (bf16[4,2,16,512]{3,2,1,0:T(8,128)(2,1)S(1)}, bf16[4,2,16,512]{3,2,1,0:T(8,128)(2,1)}, u32[]{:S(2)}, u32[]{:S(2)}) collective-permute-start(bf16[4,2,16,512]{3,2,1,0:T(8,128)(2,1)S(1)} %bitcast.172), channel_id=1, source_target_pairs={{0,3},{1,2},{2,1},{3,0},{4,7},{5,6},{6,5},{7,4},{8,11},{9,10},{10,... | collective-permute-start | bytes 393224 | tf_op jit(solution)/shard_map/ppermute | solution.py:140
  25.1 18.9 %collective-permute-start.3 = (bf16[4,2,16,512]{3,2,1,0:T(8,128)(2,1)S(1)}, bf16[4,2,16,512]{3,2,1,0:T(8,128)(2,1)}, u32[]{:S(2)}, u32[]{:S(2)}) collective-permute-start(bf16[4,2,16,512]{3,2,1,0:T(8,128)(2,1)S(1)} %bitcast.171), channel_id=1, source_target_pairs={{0,4},{1,5},{2,6},{3,7},{4,0},{5,1},{6,2},{7,3},{8,12},{9,13},{10,... | collective-permute-start | bytes 393224 | tf_op jit(solution)/shard_map/ppermute | solution.py:140
  27.0 17.9 %collective-permute-start.4 = (bf16[4,2,16,512]{3,2,1,0:T(8,128)(2,1)S(1)}, bf16[4,2,16,512]{3,2,1,0:T(8,128)(2,1)}, u32[]{:S(2)}, u32[]{:S(2)}) collective-permute-start(bf16[4,2,16,512]{3,2,1,0:T(8,128)(2,1)S(1)} %bitcast.170), channel_id=1, source_target_pairs={{0,5},{1,4},{2,7},{3,6},{4,1},{5,0},{6,3},{7,2},{8,13},{9,12},{10,... | collective-permute-start | bytes 393224 | tf_op jit(solution)/shard_map/ppermute | solution.py:140
  38.6 9.1 %collective-permute-start.5 = (bf16[4,2,16,512]{3,2,1,0:T(8,128)(2,1)}, bf16[4,2,16,512]{3,2,1,0:T(8,128)(2,1)S(1)}, u32[]{:S(2)}, u32[]{:S(2)}) collective-permute-start(bf16[4,2,16,512]{3,2,1,0:T(8,128)(2,1)} %bitcast.175), channel_id=1, source_target_pairs={{0,6},{1,7},{2,4},{3,5},{4,2},{5,3},{6,0},{7,1},{8,14},{9,15},{10,... | collective-permute-start | bytes 393224 | tf_op jit(solution)/shard_map/ppermute | solution.py:140
  42.0 11.2 %collective-permute-start.6 = (bf16[4,2,16,512]{3,2,1,0:T(8,128)(2,1)}, bf16[4,2,16,512]{3,2,1,0:T(8,128)(2,1)S(1)}, u32[]{:S(2)}, u32[]{:S(2)}) collective-permute-start(bf16[4,2,16,512]{3,2,1,0:T(8,128)(2,1)} %bitcast.174), channel_id=1, source_target_pairs={{0,7},{1,6},{2,5},{3,4},{4,3},{5,2},{6,1},{7,0},{8,15},{9,14},{10,... | collective-permute-start | bytes 393224 | tf_op jit(solution)/shard_map/ppermute | solution.py:140
  115.6 48.7 %copy-start.3 = (bf16[32,5120]{1,0:T(8,128)(2,1)S(1)}, bf16[32,5120]{1,0:T(8,128)(2,1)}, u32[]{:S(2)}) copy-start(bf16[32,5120]{1,0:T(8,128)(2,1)} %param.16) | copy-start | bytes 983044
  115.6 48.7 %copy-start.28 = (f32[1,1,5120]{2,0,1:T(1,128)S(1)}, f32[1,1,5120]{2,0,1:T(1,128)}, u32[]{:S(2)}) copy-start(f32[1,1,5120]{2,0,1:T(1,128)} %get-tuple-element.48) | copy-start | bytes 61444
  115.6 48.7 %copy-start.31 = (pred[32]{0:T(512)(128)(4,1)S(1)}, pred[32]{0:T(512)(128)(4,1)}, u32[]{:S(2)}) copy-start(pred[32]{0:T(512)(128)(4,1)} %copy-done.30) | copy-start | bytes 100
  115.7 48.7 %copy-start.33 = (pred[32]{0:T(512)(128)(4,1)S(1)}, pred[32]{0:T(512)(128)(4,1)}, u32[]{:S(2)}) copy-start(pred[32]{0:T(512)(128)(4,1)} %copy-done.32) | copy-start | bytes 100
  121.2 44.8 %copy-start.29 = (f32[5120]{0:T(1024)S(1)}, f32[5120]{0:T(1024)}, u32[]{:S(2)}) copy-start(f32[5120]{0:T(1024)} %param.28) | copy-start | bytes 61444
  121.3 75.9 %all-gather.8.cloned.1.call-start = ((), (), s32[]{:S(2)}) async-start(), calls=%async_computation.5 | async-start | bytes 2949120 | tf_op jit(solution)/shard_map/all_gather | solution.py:118
  166.9 108.7 %reduce-scatter.6.cloned.1.call-start = ((), (), s32[]{:S(2)}) async-start(), calls=%async_computation.6 | async-start | bytes 2949120 | tf_op jit(solution)/shard_map/reduce_scatter | solution.py:121
  231.7 45.3 %copy-start.18 = (f32[1,1,5120]{2,0,1:T(1,128)S(1)}, f32[1,1,5120]{2,0,1:T(1,128)}, u32[]{:S(2)}) copy-start(f32[1,1,5120]{2,0,1:T(1,128)} %get-tuple-element.31) | copy-start | bytes 61444
  231.7 45.3 %copy-start.19 = (f32[1,1,5120]{2,0,1:T(1,128)S(1)}, f32[1,1,5120]{2,0,1:T(1,128)}, u32[]{:S(2)}) copy-start(f32[1,1,5120]{2,0,1:T(1,128)} %get-tuple-element.32) | copy-start | bytes 61444
  231.7 45.4 %copy-start.20 = (f32[1,1,5120]{2,0,1:T(1,128)S(1)}, f32[1,1,5120]{2,0,1:T(1,128)}, u32[]{:S(2)}) copy-start(f32[1,1,5120]{2,0,1:T(1,128)} %get-tuple-element.33) | copy-start | bytes 61444
  231.7 45.4 %copy-start.21 = (f32[1,1,5120]{2,0,1:T(1,128)S(1)}, f32[1,1,5120]{2,0,1:T(1,128)}, u32[]{:S(2)}) copy-start(f32[1,1,5120]{2,0,1:T(1,128)} %get-tuple-element.34) | copy-start | bytes 61444
  231.7 45.4 %copy-start.22 = (f32[1,1,5120]{2,0,1:T(1,128)S(1)}, f32[1,1,5120]{2,0,1:T(1,128)}, u32[]{:S(2)}) copy-start(f32[1,1,5120]{2,0,1:T(1,128)} %get-tuple-element.35) | copy-start | bytes 61444
  231.8 45.4 %copy-start.23 = (f32[1,1,5120]{2,0,1:T(1,128)S(1)}, f32[1,1,5120]{2,0,1:T(1,128)}, u32[]{:S(2)}) copy-start(f32[1,1,5120]{2,0,1:T(1,128)} %get-tuple-element.36) | copy-start | bytes 61444
  231.8 185.8 %all-gather.12.cloned.1.call-start = ((), (), s32[]{:S(2)}) async-start(), calls=%async_computation.8 | async-start | bytes 13107200 | tf_op jit(solution)/shard_map/all_gather | solution.py:132
  232.4 368.7 %all-gather.14.cloned.1.call-start = ((), (), s32[]{:S(2)}) async-start(), calls=%async_computation.9 | async-start | bytes 13107200 | tf_op jit(solution)/shard_map/all_gather | solution.py:133
  233.0 398.6 %all-gather.10.cloned.1.call-start = ((), (), s32[]{:S(2)}) async-start(), calls=%async_computation.7 | async-start | bytes 2949120 | tf_op jit(solution)/shard_map/all_gather | solution.py:118
  278.3 368.3 %copy-start.40 = (s32[1,16]{1,0:T(1,128)S(1)}, s32[1,16]{1,0:T(1,128)}, u32[]{:S(2)}) copy-start(s32[1,16]{1,0:T(1,128)} %param.26) | copy-start | bytes 196
  278.3 368.3 %copy-start.8 = (bf16[256,4,128]{2,0,1:T(8,128)(2,1)S(1)}, bf16[256,4,128]{2,0,1:T(8,128)(2,1)}, u32[]{:S(2)}) copy-start(bf16[256,4,128]{2,0,1:T(8,128)(2,1)} %copy-done.7) | copy-start | bytes 786436
  278.3 368.7 %copy-start.6 = (bf16[256,512]{1,0:T(8,128)(2,1)S(1)}, bf16[256,512]{1,0:T(8,128)(2,1)}, u32[]{:S(2)}) copy-start(bf16[256,512]{1,0:T(8,128)(2,1)} %copy-done.5) | copy-start | bytes 786436
  278.3 412.1 %reduce-scatter.8.cloned.1.call-start = ((), (), s32[]{:S(2)}) async-start(), calls=%async_computation.10 | async-start | bytes 2949120 | tf_op jit(solution)/shard_map/reduce_scatter | solution.py:121
  646.5 45.9 %copy-start.1 = (bf16[4,5120,32]{1,2,0:T(8,128)(2,1)S(1)}, bf16[4,5120,32]{1,2,0:T(8,128)(2,1)}, u32[]{:S(2)}) copy-start(bf16[4,5120,32]{1,2,0:T(8,128)(2,1)} %param.21) | copy-start | bytes 3932164
  648.3 44.1 %copy-start.11 = (bf16[2,16,16,512]{3,2,1,0:T(8,128)(2,1)}, bf16[2,16,16,512]{3,2,1,0:T(8,128)(2,1)S(1)}, u32[]{:S(2)}) copy-start(bf16[2,16,16,512]{3,2,1,0:T(8,128)(2,1)S(1)} %scatter_fusion) | copy-start | bytes 1572868
  (27 other events, 443.5 us)
Sparse Core Ops, SparseCore 0:
  16.5 40.5 all-gather.5
  121.4 42.9 reduce-scatter.3
  167.1 30.0 all-gather.7
  231.9 43.6 reduce-scatter.5
  646.7 43.6 reduce-scatter.7
Sparse Core Ops, SparseCore 1:
  233.8 183.7 all-gather.11
  419.1 181.9 all-gather.13
  603.4 28.1 all-gather.9
